TPU v7x, 512 devices: a whole 4x8x8 slice. The times are simulated.
512 devices in a mesh: dp: 32 (over z, y_lo, core), tensor: 16 (over y_hi, x).
Axes of the slice: x: 4, y: 8 (y_hi: 4, y_lo: 2; y = y_hi * 2 + y_lo), z: 8, core: 2. Of those that a mesh axis runs over, the one named last changes fastest.
Arguments:
- tokens: bfloat16 [3072, 8192], P('tensor', 'dp'), may hold values from -6 to 6
- w_gate: bfloat16 [8192, 26624], P('dp', 'tensor'), may hold values from -0.0625 to 0.0625
- gate_pre: bfloat16 [3072, 26624], P('dp', 'tensor'), may hold values from -8 to 8
- up_act: bfloat16 [3072, 26624], P('dp', 'tensor'), may hold values from -6 to 6
- d_hidden: bfloat16 [3072, 26624], P('dp', 'tensor'), may hold values from -6 to 6
- block_mask: int32 [64, 208, 8], P('dp', 'tensor'), may hold values 0 or 1
- lang_ids: int32 [3072], P('tensor'), may hold values from 0 to 7
Outputs:
- input_grad: bfloat16 [3072, 8192], P('tensor', 'dp')
- weight_grad: float32 [8192, 26624], P('dp', 'tensor')
All inputs are finite; a program needn't handle non-finite values. No bound on the sum of `block_mask` on one device may be relied on, other than what follows from the above.
Results may differ from a plain program's by a relative error of at most 0.0049.
Values may be sent and summed in bfloat16 or wider, within the bound.
A program may use at most 128 MiB of HBM per device.

v0:
```python
import jax
import jax.numpy as jnp
from jax import lax
from jax.sharding import PartitionSpec as P


def lookup_masks(language_ids, block_mask):
    language_count = block_mask.shape[2]
    onehot = (language_ids[:, None] == jnp.arange(language_count, dtype=jnp.int32)[None, :]).astype(
        jnp.bfloat16
    )
    table = block_mask.astype(jnp.bfloat16)
    return jnp.einsum("nl,kjl->nkj", onehot, table, preferred_element_type=jnp.float32).astype(
        jnp.bfloat16
    )


def input_rows_of(gradients, mask_rows, w_blocks):
    row_count = gradients.shape[0]
    row_blocks, block_size, col_blocks, _ = w_blocks.shape
    shaped = gradients.reshape(row_count, col_blocks, block_size)

    def input_one_rowblock(block_index):
        mask_part = lax.dynamic_index_in_dim(mask_rows, block_index, 1, keepdims=False)
        scaled = shaped * mask_part[:, :, None]
        w_part = lax.dynamic_index_in_dim(w_blocks, block_index, 0, keepdims=False)
        return jnp.einsum("njf,djf->nd", scaled, w_part, preferred_element_type=jnp.float32)

    parts = lax.map(input_one_rowblock, jnp.arange(row_blocks, dtype=jnp.int32))
    return jnp.transpose(parts, (1, 0, 2)).reshape(row_count, row_blocks * block_size)


def weight_product(row_data, gradients, mask_rows):
    row_count = row_data.shape[0]
    row_blocks = mask_rows.shape[1]
    col_blocks = mask_rows.shape[2]
    block_size = row_data.shape[1] // row_blocks
    shaped = gradients.reshape(row_count, col_blocks, block_size)

    def weight_one_rowblock(block_index):
        mask_part = lax.dynamic_index_in_dim(mask_rows, block_index, 1, keepdims=False)
        scaled = shaped * mask_part[:, :, None]
        data_part = lax.dynamic_slice_in_dim(row_data, block_index * block_size, block_size, 1)
        return jnp.einsum("nd,njf->djf", data_part, scaled, preferred_element_type=jnp.float32)

    parts = lax.map(weight_one_rowblock, jnp.arange(row_blocks, dtype=jnp.int32))
    return parts.reshape(row_blocks * block_size, col_blocks * block_size)


def local(tokens, w_gate, gate_pre, up_act, d_hidden, block_mask, lang_ids):
    gate_value = gate_pre.astype(jnp.float32)
    sigmoid_gate = jax.nn.sigmoid(gate_value)
    gate_grad = (
        d_hidden.astype(jnp.float32)
        * up_act.astype(jnp.float32)
        * sigmoid_gate
        * (1.0 + gate_value * (1.0 - sigmoid_gate))
    ).astype(jnp.bfloat16)
    all_rows, all_ids = (
        lax.all_gather(tokens, "tensor", axis=0, tiled=True),
        lax.all_gather(lang_ids, "tensor", axis=0, tiled=True),
    )
    token_count = all_rows.shape[0]
    row_blocks = block_mask.shape[0]
    col_blocks = block_mask.shape[1]
    block_size = w_gate.shape[0] // row_blocks
    w_blocks = w_gate.reshape(row_blocks, block_size, col_blocks, block_size)
    arrived = lax.all_gather(gate_grad, "dp", axis=0, tiled=True)
    mask_rows = lookup_masks(all_ids, block_mask)
    weights_sum = weight_product(all_rows, arrived, mask_rows)
    updated = input_rows_of(arrived, mask_rows, w_blocks)
    partial_value = updated
    weights_sum, partial_value = (weights_sum, partial_value)
    input_grad = lax.psum_scatter(partial_value, "tensor", scatter_dimension=0, tiled=True)
    weight_grad = weights_sum / jnp.sqrt(jnp.float32(token_count))
    return (input_grad.astype(jnp.bfloat16), weight_grad)


def solution(mesh):
    placed = (
        P("tensor", "dp"),
        P("dp", "tensor"),
        P("dp", "tensor"),
        P("dp", "tensor"),
        P("dp", "tensor"),
        P("dp", "tensor", None),
        P("tensor"),
    )
    return jax.shard_map(
        local,
        mesh=mesh,
        in_specs=placed,
        out_specs=(P("tensor", "dp"), P("dp", "tensor")),
        check_vma=False,
    )
```

profile of v0, /device:TPU:64, one launch (start us, length us, event | category | flops | bytes accessed | tf_op | source)
XLA Modules:
  0.0 262.1 jit_solution(4391563297279748045)
XLA Ops:
  7.2 0.0 copy-start.1
  7.2 0.0 all-gather.3.cloned.1.call-start
  7.2 2.2 fusion.29
  9.4 0.0 all-gather.3.cloned.1.call-update
  9.4 0.0 all-gather.5.cloned.1.call-start
  9.5 0.7 all-gather.5.cloned.1.call-update
  10.2 0.0 reduce-scatter.2.cloned.1.call-start
  10.3 1.3 dynamic-slice
  12.2 0.9 dynamic-update-slice
  13.1 83.0 %all-reduce = s32[3072]{0:T(1024)S(1)} all-reduce(s32[3072]{0:T(1024)S(1)} %dynamic-update-slice), channel_id=1, replica_groups=mesh['dp'=32,'tensor'=16] {'tensor'}, use_global_device_ids=true, to_apply=%add | all-reduce | flops 3072 | bytes 24576
  96.1 1.7 reshape.33
  97.8 1.1 copy.26
  98.9 0.0 copy-done.1
  98.9 0.2 convolution_convert_fusion
  99.2 0.0 all-gather.3.cloned.1.call-done
  99.2 14.3 %copy.23 = bf16[3072,1664]{0,1:T(8,128)(2,1)} copy(bf16[3072,1664]{1,0:T(8,128)(2,1)} %all-gather.3.cloned.1.call-done) | data formatting | bytes 20447232 | tf_op jit(solution)/shard_map/all_gather | solution.py:68
  113.5 0.0 copy-start
  113.5 14.4 %copy.25 = bf16[3072,13,128]{2,0,1:T(8,128)(2,1)} copy(bf16[3072,13,128]{0,2,1:T(8,128)(2,1)} %bitcast.54) | data formatting | bytes 20447232 | tf_op jit(solution)/shard_map/while | solution.py:29
  127.9 0.0 copy-done
  127.9 25.5 %while.20 = (s32[]{:T(128)}, f32[2,3072,128]{2,1,0:T(8,128)S(1)}, s32[2]{0:T(128)S(1)}, bf16[3072,2,13]{0,2,1:T(8,128)(2,1)S(1)}, bf16[3072,13,128]{2,0,1:T(8,12...) while((s32[]{:T(128)}, f32[2,3072,128]{2,1,0:T(8,128)S(1)}, ...), condition=%wide.region_1.2_spmd, body=%wide.region_0.1_spmd.sunk | while | flops 1313734656 | bytes 12481171 | solution.py:29
  127.9 0.7 dynamic_slice.39
  130.7 9.9 %fusion.43 = f32[2,3072,128]{2,1,0:T(8,128)S(1)} fusion(f32[2,3072,128]{2,1,0:T(8,128)S(1)} %get-tuple-element.204, s32[]{:T(128)} %get-tuple-element.203, bf16[3072,13,128]{2,0,1:T(8,128)(2,1)} %get-tuple-element.216, bf16[3072,13]{0,1:T(8,128)(2,1)S(1)} %dynamic-slice_bitcast_fusion.4, bf16[2,128,13,128]{3,1,2,0:T(8,128)(2,1)} %get-tuple-element.217, ...), kind=kOutput, calls=%fused_computation.4.clone.1 | convolution fusion | flops 1313734656 | bytes 12321284 | tf_op jit(solution)/shard_map/while/body/eval_jaxpr/njf,djf->nd/dot_general | solution.py:27
  140.6 0.7 dynamic_slice.39
  143.4 10.0 %fusion.43 = f32[2,3072,128]{2,1,0:T(8,128)S(1)} fusion(f32[2,3072,128]{2,1,0:T(8,128)S(1)} %get-tuple-element.204, s32[]{:T(128)} %get-tuple-element.203, bf16[3072,13,128]{2,0,1:T(8,128)(2,1)} %get-tuple-element.216, bf16[3072,13]{0,1:T(8,128)(2,1)S(1)} %dynamic-slice_bitcast_fusion.4, bf16[2,128,13,128]{3,1,2,0:T(8,128)(2,1)} %get-tuple-element.217, ...), kind=kOutput, calls=%fused_computation.4.clone.1 | convolution fusion | flops 1313734656 | bytes 12321284 | tf_op jit(solution)/shard_map/while/body/eval_jaxpr/njf,djf->nd/dot_general | solution.py:27
  153.4 2.0 copy_bitcast_fusion
  155.4 0.0 reduce-scatter.2.cloned.1.call-update
  155.4 0.0 all-gather.5.cloned.1.call-done
  155.5 34.0 %while.21 = (s32[]{:T(128)}, f32[2,128,13,128]{3,1,2,0:T(8,128)S(1)}, s32[2]{0:T(128)S(1)}, bf16[3072,256]{1,0:T(8,128)(2,1)}, bf16[3072,2,13]{0,2,1:T(8,128)(2,...) while((s32[]{:T(128)}, ...), condition=%wide.region_4.5_spmd, body=%wide.region_3.4_spmd.sunk | while | flops 1329070080 | bytes 12120785 | solution.py:46
  155.5 0.6 dynamic_slice.42
  158.7 13.8 %fusion.46 = f32[2,128,13,128]{3,1,2,0:T(8,128)S(1)} fusion(f32[2,128,13,128]{3,1,2,0:T(8,128)S(1)} %get-tuple-element.233, s32[]{:T(128)} %get-tuple-element.232, bf16[3072,13,128]{2,0,1:T(8,128)(2,1)} %get-tuple-element.248, bf16[3072,13]{0,1:T(8,128)(2,1)S(1)} %dynamic-slice_bitcast_fusion.5, bf16[3072,256]{1,0:T(8,128)(2,1)} %get-tuple-element.246, ...), kind=kOutput, calls=%fused_computation.13.clone.1 | convolution fusion | flops 1329070080 | bytes 11960836 | tf_op jit(solution)/shard_map/while/body/eval_jaxpr/nd,njf->djf/dot_general | solution.py:44
  172.5 0.6 dynamic_slice.42
  175.7 13.8 %fusion.46 = f32[2,128,13,128]{3,1,2,0:T(8,128)S(1)} fusion(f32[2,128,13,128]{3,1,2,0:T(8,128)S(1)} %get-tuple-element.233, s32[]{:T(128)} %get-tuple-element.232, bf16[3072,13,128]{2,0,1:T(8,128)(2,1)} %get-tuple-element.248, bf16[3072,13]{0,1:T(8,128)(2,1)S(1)} %dynamic-slice_bitcast_fusion.5, bf16[3072,256]{1,0:T(8,128)(2,1)} %get-tuple-element.246, ...), kind=kOutput, calls=%fused_computation.13.clone.1 | convolution fusion | flops 1329070080 | bytes 11960836 | tf_op jit(solution)/shard_map/while/body/eval_jaxpr/nd,njf->djf/dot_general | solution.py:44
  189.4 0.2 broadcast_multiply_fusion
  189.6 1.0 copy.34
  190.6 1.9 copy.41
  192.5 61.5 %reduce-scatter.2.cloned.1.call-done = f32[192,256]{1,0:T(8,128)} async-done(((f32[3072,256]{1,0:T(8,128)}), f32[192,256]{1,0:T(8,128)}) %reduce-scatter.2.cloned.1.call-update) | async-done | bytes 196624 | tf_op jit(solution)/shard_map/reduce_scatter | solution.py:74
  254.0 1.6 convert_element_type.28
  (9 shorter events, 0.1 us)
Async XLA Ops:
  7.2 91.8 %copy-start.1 = (s32[2,13,8]{1,2,0:T(8,128)S(1)}, s32[2,13,8]{1,2,0:T(8,128)}, u32[]{:S(2)}) copy-start(s32[2,13,8]{1,2,0:T(8,128)} %param.16) | copy-start | bytes 2500
  7.2 92.0 %all-gather.3.cloned.1.call-start = ((), (), s32[]{:S(2)}) async-start(), calls=%async_computation.1 | async-start | bytes 10543104 | tf_op jit(solution)/shard_map/all_gather | solution.py:68
  9.4 146.0 %all-gather.5.cloned.1.call-start = ((), (), s32[]{:S(2)}) async-start(), calls=%async_computation.3 | async-start | bytes 1671168 | tf_op jit(solution)/shard_map/all_gather | solution.py:60
  10.2 243.8 %reduce-scatter.2.cloned.1.call-start = ((), (), s32[]{:S(2)}) async-start(), calls=%async_computation.2 | async-start | bytes 3342336 | tf_op jit(solution)/shard_map/reduce_scatter | solution.py:74
  113.5 14.4 %copy-start = (f32[2,3072,128]{2,1,0:T(8,128)S(1)}, f32[2,3072,128]{2,1,0:T(8,128)}, u32[]{:S(2)}) copy-start(f32[2,3072,128]{2,1,0:T(8,128)} %custom-call) | copy-start | bytes 9437188
Sparse Core Ops, SparseCore 0:
  10.2 80.9 all-gather.2
  94.2 60.6 all-gather.4
  159.0 94.9 reduce-scatter.1
where the time goes:
time: 263 us; the launch traced here: 262 us
  blocking collectives  83 us (32%)
  waiting for transfers between devices  62.3 us (24%)
  matrix products  47.6 us (18%)
  local copies, waits for them, and re-layouts  41.2 us (16%)
  between operations  14.5 us (6%)
  loops' own time  9.45 us (4%)
  other arithmetic  3.92 us (1%)
    unnamed x1, blocking collectives  83 us
    reduce_scatter x1, waiting for transfers between devices, local(): lax.psum_scatter(partial_value, 'tensor', scatter_dimension=0, tiled=True)  61.5 us
    dot_general x2, matrix products, weight_one_rowblock(): jnp.einsum('nd,njf->djf', data_part, scaled, preferred_element_type=jnp.f...  27.5 us
    dot_general x2, matrix products, input_one_rowblock(): jnp.einsum('njf,djf->nd', scaled, w_part, preferred_element_type=jnp.floa...  19.9 us
    while x2, local copies, waits for them, and re-layouts, input_rows_of(): parts = lax.map(input_one_rowblock, jnp.arange(row_blocks, dtype=jnp.int32))  15.5 us
    all_gather x1, local copies, waits for them, and re-layouts, local(): arrived = lax.all_gather(gate_grad, 'dp', axis=0, tiled=True)  14.3 us
  transfers between devices with their start and end apart: 3, of which 1 were waited for; matrix products, arithmetic and copies ran while one was open for 34% of the time, Pallas kernels for 0%

commit v1 on v0

--- a/solution.py
+++ b/solution.py
@@ -65,7 +65,9 @@
     col_blocks = block_mask.shape[1]
     block_size = w_gate.shape[0] // row_blocks
     w_blocks = w_gate.reshape(row_blocks, block_size, col_blocks, block_size)
-    arrived = lax.all_gather(gate_grad, "dp", axis=0, tiled=True)
+    arrived = jnp.concatenate(
+        lax.all_to_all(jnp.stack([gate_grad] * lax.axis_size("dp")), "dp", 0, 0), axis=0
+    )
     mask_rows = lookup_masks(all_ids, block_mask)
     weights_sum = weight_product(all_rows, arrived, mask_rows)
     updated = input_rows_of(arrived, mask_rows, w_blocks)

time: 263 us -> 471 us (1.79)
  blocking collectives: 83 us -> 269 us
  starting transfers between devices: 0.12 us -> 11.4 us
  waiting for transfers between devices: 62.3 us -> 67.9 us
  local copies, waits for them, and re-layouts: 41.2 us -> 46.4 us
    unnamed x1, blocking collectives: 83 us -> 269 us
    another operation x0 -> x2, local copies, waits for them, and re-layouts: none -> 23.4 us  [the longest x1 18.8 us: input_rows_of(): shaped = gradients.reshape(row_count, col_blocks, block_size)]
    all_gather x1 -> x0, local copies, waits for them, and re-layouts: 14.3 us -> none  [local(): arrived = lax.all_gather(gate_grad, 'dp', axis=0, tiled=True)]
    all_to_all x0 -> x1, starting transfers between devices: none -> 11.3 us  [local(): lax.all_to_all(jnp.stack([gate_grad] * lax.axis_size('dp')), 'dp', 0, 0)]
    reduce_scatter x1, waiting for transfers between devices: 61.5 us -> 67.2 us  [local(): lax.psum_scatter(partial_value, 'tensor', scatter_dimension=0, tiled=True)]
  transfers between devices with their start and end apart: 3 -> 3, of which waited for: 1 -> 1; matrix products, arithmetic and copies ran while one was open for 34% -> 19% of each run, Pallas kernels for 0% -> 0%
where the time goes in v1:
time: 471 us; the launch traced here: 470 us
  blocking collectives  269 us (57%)
  waiting for transfers between devices  67.9 us (14%)
  matrix products  47.8 us (10%)
  local copies, waits for them, and re-layouts  46.4 us (10%)
  between operations  14.7 us (3%)
  starting transfers between devices  11.4 us (2%)
  loops' own time  9.45 us (2%)
    unnamed x1, blocking collectives  269 us
    reduce_scatter x1, waiting for transfers between devices, local(): lax.psum_scatter(partial_value, 'tensor', scatter_dimension=0, tiled=True)  67.2 us
    dot_general x2, matrix products, weight_one_rowblock(): jnp.einsum('nd,njf->djf', data_part, scaled, preferred_element_type=jnp.f...  27.6 us
    dot_general x2, matrix products, input_one_rowblock(): jnp.einsum('njf,djf->nd', scaled, w_part, preferred_element_type=jnp.floa...  19.9 us
    another operation x1, local copies, waits for them, and re-layouts, input_rows_of(): shaped = gradients.reshape(row_count, col_blocks, block_size)  18.8 us
    while x2, local copies, waits for them, and re-layouts, input_rows_of(): parts = lax.map(input_one_rowblock, jnp.arange(row_blocks, dtype=jnp.int32))  13.5 us
    all_to_all x1, starting transfers between devices, local(): lax.all_to_all(jnp.stack([gate_grad] * lax.axis_size('dp')), 'dp', 0, 0)  11.3 us
  transfers between devices with their start and end apart: 3, of which 1 were waited for; matrix products, arithmetic and copies ran while one was open for 19% of the time, Pallas kernels for 0%

profile of v1, /device:TPU:64, one launch (start us, length us, event | category | flops | bytes accessed | tf_op | source)
XLA Modules:
  0.0 469.7 jit_solution(88831051793891250)
XLA Ops:
  7.2 1.5 fusion.29
  8.6 4.6 stack.2
  13.2 0.0 copy-start.1
  13.2 11.3 %all-to-all-start = ((bf16[32,96,1664]{2,1,0:T(8,128)(2,1)}), bf16[32,96,1664]{2,1,0:T(8,128)(2,1)}, u32[]{:S(2)}, u32[]{:S(2)}) async-start(bf16[32,96,1664]{2,1,0:T(8,128)(2,1)} %stack.2), calls=%async_computation | async-start | bytes 20447232 | tf_op jit(solution)/shard_map/all_to_all | solution.py:69
  24.5 0.0 copy-start.3
  24.6 0.0 copy-start.2
  24.6 0.0 all-gather.2.cloned.1.call-start
  24.6 0.7 all-gather.2.cloned.1.call-update
  25.3 0.0 reduce-scatter.2.cloned.1.call-start
  25.4 0.0 copy-done.1
  25.4 0.6 reshape.30
  26.0 1.1 copy.22
  27.1 1.3 dynamic-slice
  29.0 0.0 copy-done.3
  29.0 0.3 dynamic-update-slice
  29.3 268.8 %all-reduce = s32[3072]{0:T(1024)S(1)} all-reduce(s32[3072]{0:T(1024)S(1)} %dynamic-update-slice), channel_id=1, replica_groups=mesh['dp'=32,'tensor'=16] {'tensor'}, use_global_device_ids=true, to_apply=%add | all-reduce | flops 3072 | bytes 24576
  298.1 0.0 copy-done.2
  298.1 0.2 convolution_convert_fusion
  298.3 0.0 all-to-all-done
  298.3 18.8 %reshape_reshape.4 = bf16[3072,13,128]{2,1,0:T(8,128)(2,1)} reshape(bf16[32,96,1664]{2,1,0:T(8,128)(2,1)} %all-to-all-done) | data formatting | bytes 20447232 | tf_op jit(solution)/shard_map/reshape;reshape | solution.py:21
  317.2 0.0 copy-start
  317.2 12.3 %copy.21 = bf16[3072,13,128]{2,0,1:T(8,128)(2,1)} copy(bf16[3072,13,128]{2,1,0:T(8,128)(2,1)} %reshape_reshape.4) | data formatting | bytes 20447232 | tf_op jit(solution)/shard_map/while | solution.py:29
  329.5 0.0 copy-done
  329.5 25.4 %while.20 = (s32[]{:T(128)}, f32[2,3072,128]{2,1,0:T(8,128)S(1)}, s32[2]{0:T(128)S(1)}, bf16[3072,2,13]{0,2,1:T(8,128)(2,1)S(1)}, bf16[3072,13,128]{2,0,1:T(8,12...) while((s32[]{:T(128)}, f32[2,3072,128]{2,1,0:T(8,128)S(1)}, ...), condition=%wide.region_1.2_spmd, body=%wide.region_0.1_spmd.sunk | while | flops 1313734656 | bytes 12481171 | solution.py:29
  329.5 0.7 dynamic_slice.39
  332.3 9.9 %fusion.43 = f32[2,3072,128]{2,1,0:T(8,128)S(1)} fusion(f32[2,3072,128]{2,1,0:T(8,128)S(1)} %get-tuple-element.204, s32[]{:T(128)} %get-tuple-element.203, bf16[3072,13,128]{2,0,1:T(8,128)(2,1)} %get-tuple-element.216, bf16[3072,13]{0,1:T(8,128)(2,1)S(1)} %dynamic-slice_bitcast_fusion.4, bf16[2,128,13,128]{3,1,2,0:T(8,128)(2,1)} %get-tuple-element.217, ...), kind=kOutput, calls=%fused_computation.4.clone.1 | convolution fusion | flops 1313734656 | bytes 12321284 | tf_op jit(solution)/shard_map/while/body/eval_jaxpr/njf,djf->nd/dot_general | solution.py:27
  342.2 0.7 dynamic_slice.39
  345.0 9.9 %fusion.43 = f32[2,3072,128]{2,1,0:T(8,128)S(1)} fusion(f32[2,3072,128]{2,1,0:T(8,128)S(1)} %get-tuple-element.204, s32[]{:T(128)} %get-tuple-element.203, bf16[3072,13,128]{2,0,1:T(8,128)(2,1)} %get-tuple-element.216, bf16[3072,13]{0,1:T(8,128)(2,1)S(1)} %dynamic-slice_bitcast_fusion.4, bf16[2,128,13,128]{3,1,2,0:T(8,128)(2,1)} %get-tuple-element.217, ...), kind=kOutput, calls=%fused_computation.4.clone.1 | convolution fusion | flops 1313734656 | bytes 12321284 | tf_op jit(solution)/shard_map/while/body/eval_jaxpr/njf,djf->nd/dot_general | solution.py:27
  355.0 1.9 copy_bitcast_fusion
  356.8 0.0 reduce-scatter.2.cloned.1.call-update
  356.9 0.0 all-gather.2.cloned.1.call-done
  356.9 34.1 %while.21 = (s32[]{:T(128)}, f32[2,128,13,128]{3,1,2,0:T(8,128)S(1)}, s32[2]{0:T(128)S(1)}, bf16[3072,256]{1,0:T(8,128)(2,1)}, bf16[3072,2,13]{0,2,1:T(8,128)(2,...) while((s32[]{:T(128)}, ...), condition=%wide.region_4.5_spmd, body=%wide.region_3.4_spmd.sunk | while | flops 1329070080 | bytes 12120785 | solution.py:46
  356.9 0.6 dynamic_slice.42
  360.1 13.8 %fusion.46 = f32[2,128,13,128]{3,1,2,0:T(8,128)S(1)} fusion(f32[2,128,13,128]{3,1,2,0:T(8,128)S(1)} %get-tuple-element.233, s32[]{:T(128)} %get-tuple-element.232, bf16[3072,13,128]{2,0,1:T(8,128)(2,1)} %get-tuple-element.248, bf16[3072,13]{0,1:T(8,128)(2,1)S(1)} %dynamic-slice_bitcast_fusion.5, bf16[3072,256]{1,0:T(8,128)(2,1)} %get-tuple-element.246, ...), kind=kOutput, calls=%fused_computation.13.clone.1 | convolution fusion | flops 1329070080 | bytes 11960836 | tf_op jit(solution)/shard_map/while/body/eval_jaxpr/nd,njf->djf/dot_general | solution.py:44
  373.9 0.6 dynamic_slice.42
  377.1 13.9 %fusion.46 = f32[2,128,13,128]{3,1,2,0:T(8,128)S(1)} fusion(f32[2,128,13,128]{3,1,2,0:T(8,128)S(1)} %get-tuple-element.233, s32[]{:T(128)} %get-tuple-element.232, bf16[3072,13,128]{2,0,1:T(8,128)(2,1)} %get-tuple-element.248, bf16[3072,13]{0,1:T(8,128)(2,1)S(1)} %dynamic-slice_bitcast_fusion.5, bf16[3072,256]{1,0:T(8,128)(2,1)} %get-tuple-element.246, ...), kind=kOutput, calls=%fused_computation.13.clone.1 | convolution fusion | flops 1329070080 | bytes 11960836 | tf_op jit(solution)/shard_map/while/body/eval_jaxpr/nd,njf->djf/dot_general | solution.py:44
  391.0 0.2 broadcast_multiply_fusion
  391.2 1.0 copy.30
  392.2 1.9 copy.37
  394.1 67.2 %reduce-scatter.2.cloned.1.call-done = f32[192,256]{1,0:T(8,128)} async-done(((f32[3072,256]{1,0:T(8,128)}), f32[192,256]{1,0:T(8,128)}) %reduce-scatter.2.cloned.1.call-update) | async-done | bytes 196624 | tf_op jit(solution)/shard_map/reduce_scatter | solution.py:76
  461.3 1.6 convert_element_type.28
  (9 shorter events, 0.1 us)
Async XLA Ops:
  13.2 12.2 %copy-start.1 = (bf16[256,1664]{1,0:T(8,128)(2,1)S(1)}, bf16[256,1664]{1,0:T(8,128)(2,1)}, u32[]{:S(2)}) copy-start(bf16[256,1664]{1,0:T(8,128)(2,1)} %param.12) | copy-start | bytes 2555908
  13.2 285.1 %all-to-all-start = ((bf16[32,96,1664]{2,1,0:T(8,128)(2,1)}), bf16[32,96,1664]{2,1,0:T(8,128)(2,1)}, u32[]{:S(2)}, u32[]{:S(2)}) async-start(bf16[32,96,1664]{2,1,0:T(8,128)(2,1)} %stack.2), calls=%async_computation | async-start | bytes 20447232 | tf_op jit(solution)/shard_map/all_to_all | solution.py:69
  24.5 4.4 copy-start.3
  24.6 273.5 %copy-start.2 = (s32[2,13,8]{1,2,0:T(8,128)S(1)}, s32[2,13,8]{1,2,0:T(8,128)}, u32[]{:S(2)}) copy-start(s32[2,13,8]{1,2,0:T(8,128)} %param.16) | copy-start | bytes 2500
  24.6 332.3 %all-gather.2.cloned.1.call-start = ((), (), s32[]{:S(2)}) async-start(), calls=%async_computation.3 | async-start | bytes 1671168 | tf_op jit(solution)/shard_map/all_gather | solution.py:60
  25.3 436.0 %reduce-scatter.2.cloned.1.call-start = ((), (), s32[]{:S(2)}) async-start(), calls=%async_computation.2 | async-start | bytes 3342336 | tf_op jit(solution)/shard_map/reduce_scatter | solution.py:76
  317.2 12.3 %copy-start = (f32[2,3072,128]{2,1,0:T(8,128)S(1)}, f32[2,3072,128]{2,1,0:T(8,128)}, u32[]{:S(2)}) copy-start(f32[2,3072,128]{2,1,0:T(8,128)} %custom-call) | copy-start | bytes 9437188
Sparse Core Ops, SparseCore 0:
  28.4 73.1 all-gather.1
  357.0 104.2 reduce-scatter.1
